TPU v7x, 512 devices: a whole 4x4x16 slice. The times are simulated.
512 devices in a mesh: dp: 16 (over z), row: 8 (over y, core), col: 4 (over x).
Axes of the slice: x: 4, y: 4, z: 16, core: 2. Of those that a mesh axis runs over, the one named last changes fastest.
Arguments:
- grad_blocks: bfloat16 [16, 4096, 1024], P('dp', 'row', 'col'), may hold values from -300 to 300
- ln_grads: bfloat16 [16, 4, 1024], P('dp', None, 'col'), may hold values from -240 to 240, as said below
- master: float32 [4096, 1024], P(('row', 'col')), may hold values from -6 to 6
- first_moment: float32 [4096, 1024], P(('row', 'col')), may hold values from -6 to 6
- second_moment: float32 [4096, 1024], P(('row', 'col')), may hold values from 0.3 to 3
- average: float32 [4096, 1024], P('row', 'col'), may hold values from -6 to 6
- ln_master: float32 [4, 1024], P(None, 'col'), may hold values from -6 to 6
- ln_first: float32 [4, 1024], P(None, 'col'), may hold values from -6 to 6
- ln_second: float32 [4, 1024], P(None, 'col'), may hold values from 0.3 to 3
- ln_average: float32 [4, 1024], P(None, 'col'), may hold values from -6 to 6
Outputs:
- average_new: float32 [4096, 1024], P('row', 'col')
- master_new: float32 [4096, 1024], P(('row', 'col'))
- first_new: float32 [4096, 1024], P(('row', 'col'))
- second_new: float32 [4096, 1024], P(('row', 'col'))
- ln_master_new: float32 [4, 1024], P(None, 'col')
- ln_first_new: float32 [4, 1024], P(None, 'col')
- ln_second_new: float32 [4, 1024], P(None, 'col')
- ln_average_new: float32 [4, 1024], P(None, 'col')
Inputs may be any that keep to these rules, and one draw needn't show every extreme that they name: `ln_grads`: partial gradients of each data-parallel group.
All inputs are finite; a program needn't handle non-finite values.
Results may differ from a plain program's by a relative error of at most 0.0003.
Values may be sent and summed in bfloat16 or wider, within the bound.
A program may use at most 64 MiB of HBM per device.

v0:
```python
import math
import jax
import jax.numpy as jnp
from jax import lax
from jax.sharding import PartitionSpec as P

D = 1024
FF = 4096
STEP = 20
beta_one = 0.9
beta_two = 0.95
learn_rate = 0.02
decay_rate = 0.1
epsilon = 1e-08
clip_rms = 1.0
ema_keep = 0.9


def adam_step(gradient, clip_scale, first, second, master, decay_weight):
    clipped = clip_scale * gradient
    first_new = beta_one * first + (1.0 - beta_one) * clipped
    second_new = beta_two * second + (1.0 - beta_two) * clipped * clipped
    direction = (
        first_new
        / (1.0 - beta_one**STEP)
        / (jnp.sqrt(second_new / (1.0 - beta_two**STEP)) + epsilon)
    )
    master_new = master - learn_rate * (direction + decay_weight * master)
    return (master_new, first_new, second_new)


def clip_factor(norm_total):
    return jnp.minimum(1.0, clip_rms * math.sqrt(FF * D + 4 * D) / jnp.sqrt(norm_total))


def squares(gradient, ln_gradient, row_count):
    return jnp.sum(gradient * gradient) + jnp.sum(ln_gradient * ln_gradient) / row_count


def shards(
    grad_blocks,
    ln_grads,
    master,
    first_moment,
    second_moment,
    average,
    ln_master,
    ln_first,
    ln_second,
    ln_average,
):
    row_count = float(lax.axis_size("row"))
    summed, ln_gradient = lax.psum(
        (grad_blocks[0].astype(jnp.float32), ln_grads[0].astype(jnp.float32)), "dp"
    )
    gradient = lax.all_to_all(summed, "col", split_axis=0, concat_axis=1, tiled=True)
    norm_total = lax.psum(squares(gradient, ln_gradient, row_count), ("row", "col"))
    clip_scale = clip_factor(norm_total)
    master_new, first_new, second_new = adam_step(
        gradient, clip_scale, first_moment, second_moment, master, decay_rate
    )
    ln_master_new, ln_first_new, ln_second_new = adam_step(
        ln_gradient, clip_scale, ln_first, ln_second, ln_master, 0.0
    )
    ln_average_new = ema_keep * ln_average + (1.0 - ema_keep) * ln_master_new
    block_master = lax.all_to_all(master_new, "col", split_axis=1, concat_axis=0, tiled=True)
    average_new = ema_keep * average + (1.0 - ema_keep) * block_master
    return (
        average_new,
        master_new,
        first_new,
        second_new,
        ln_master_new,
        ln_first_new,
        ln_second_new,
        ln_average_new,
    )


def solution(mesh):
    placed = (
        P("dp", "row", "col"),
        P("dp", None, "col"),
        P(("row", "col"), None),
        P(("row", "col"), None),
        P(("row", "col"), None),
        P("row", "col"),
        P(None, "col"),
        P(None, "col"),
        P(None, "col"),
        P(None, "col"),
    )
    return jax.shard_map(
        shards,
        mesh=mesh,
        in_specs=placed,
        out_specs=(
            P("row", "col"),
            P(("row", "col"), None),
            P(("row", "col"), None),
            P(("row", "col"), None),
            P(None, "col"),
            P(None, "col"),
            P(None, "col"),
            P(None, "col"),
        ),
        check_vma=False,
    )
```

profile of v0, /device:TPU:2, one launch (start us, length us, event | category | flops | bytes accessed | tf_op | source)
XLA Modules:
  0.0 162.7 jit_solution(14626310819225786435)
XLA Ops:
  0.6 0.7 bitcast_convert_fusion
  1.3 69.7 %all-reduce.2 = (f32[4,128,256]{2,1,0:T(8,128)}, f32[4,256]{1,0:T(4,128)S(1)}) all-reduce(bf16[4,128,256]{2,1,0:T(8,128)(2,1)} %bitcast.20, f32[4,256]{1,0:T(4,128)S(1)} %bitcast_convert_fusion), channel_id=1, replica_groups=mesh['dp'=16,'row'=8,'col'=4] {'dp'}, use_global_device_ids=true, to_apply=%region_0.0 | all-reduce | flops 132096 | bytes 794624 | tf_op jit(solution)/shard_map/psum | solution.py:53
  71.0 5.0 %all-to-all-start = ((f32[4,128,256]{2,1,0:T(8,128)}), f32[4,128,256]{2,1,0:T(8,128)S(1)}, u32[]{:S(2)}, u32[]{:S(2)}) async-start(f32[4,128,256]{2,1,0:T(8,128)} %get-tuple-element.16), calls=%async_computation | async-start | bytes 1048576 | tf_op jit(solution)/shard_map/all_to_all | solution.py:56
  76.0 0.0 copy-done.1
  76.0 0.2 copy.24
  76.2 0.8 copy-done.2
  77.0 0.2 copy.20
  77.2 0.0 copy-start.3
  77.2 0.6 multiply_reduce_fusion.1
  78.5 4.1 %all-to-all-done = f32[4,128,256]{2,1,0:T(8,128)S(1)} async-done(((f32[4,128,256]{2,1,0:T(8,128)}), f32[4,128,256]{2,1,0:T(8,128)S(1)}, u32[]{:S(2)}, u32[]{:S(2)}) %all-to-all-start) | async-done | bytes 524320 | tf_op jit(solution)/shard_map/all_to_all | solution.py:56
  82.6 0.7 multiply_reduce_fusion
  84.0 0.2 copy.22
  84.2 64.9 %psum.23 = f32[]{:T(128)} all-reduce(f32[]{:T(128)S(6)} %add.45), channel_id=1, replica_groups=mesh['dp'=16,'row'=8,'col'=4] {'row','col'}, use_global_device_ids=true, to_apply=%region_4.0 | all-reduce | flops 1 | bytes 8 | tf_op jit(solution)/shard_map/psum | solution.py:57
  149.8 0.2 copy.21
  150.0 0.4 multiply_subtract_fusion
  150.4 1.0 copy.25
  151.4 3.7 %all-to-all-start.1 = ((f32[128,4,256]{2,0,1:T(8,128)}), f32[128,4,256]{2,0,1:T(8,128)S(1)}, u32[]{:S(2)}, u32[]{:S(2)}) async-start(f32[128,4,256]{2,0,1:T(8,128)} %copy.25), calls=%async_computation.1 | async-start | bytes 1048576 | tf_op jit(solution)/shard_map/all_to_all | solution.py:66
  155.2 1.0 copy.26
  156.2 1.0 copy.27
  157.2 1.0 copy.28
  158.2 0.0 copy-done.7
  158.2 0.6 multiply_add_fusion
  158.8 3.0 %all-to-all-done.1 = f32[128,4,256]{2,0,1:T(8,128)S(1)} async-done(((f32[128,4,256]{2,0,1:T(8,128)}), f32[128,4,256]{2,0,1:T(8,128)S(1)}, u32[]{:S(2)}, u32[]{:S(2)}) %all-to-all-start.1) | async-done | bytes 524320 | tf_op jit(solution)/shard_map/all_to_all | solution.py:66
  161.9 0.9 bitcast_add_fusion
  (14 shorter events, 0.1 us)
Async XLA Ops:
  71.0 5.0 %copy-start.1 = (f32[128,1024]{1,0:T(8,128)S(1)}, f32[128,1024]{1,0:T(8,128)}, u32[]{:S(2)}) copy-start(f32[128,1024]{1,0:T(8,128)} %param.12) | copy-start | bytes 1572868
  71.0 11.6 %all-to-all-start = ((f32[4,128,256]{2,1,0:T(8,128)}), f32[4,128,256]{2,1,0:T(8,128)S(1)}, u32[]{:S(2)}, u32[]{:S(2)}) async-start(f32[4,128,256]{2,1,0:T(8,128)} %get-tuple-element.16), calls=%async_computation | async-start | bytes 1048576 | tf_op jit(solution)/shard_map/all_to_all | solution.py:56
  76.0 1.0 copy-start.2
  77.2 6.8 %copy-start.3 = (f32[128,1024]{1,0:T(8,128)S(1)}, f32[128,1024]{1,0:T(8,128)}, u32[]{:S(2)}) copy-start(f32[128,1024]{1,0:T(8,128)} %param.14) | copy-start | bytes 1572868
  151.4 10.4 %all-to-all-start.1 = ((f32[128,4,256]{2,0,1:T(8,128)}), f32[128,4,256]{2,0,1:T(8,128)S(1)}, u32[]{:S(2)}, u32[]{:S(2)}) async-start(f32[128,4,256]{2,0,1:T(8,128)} %copy.25), calls=%async_computation.1 | async-start | bytes 1048576 | tf_op jit(solution)/shard_map/all_to_all | solution.py:66
  157.2 1.0 copy-start.4
  157.2 1.0 copy-start.5
  157.2 1.0 copy-start.6
  157.2 1.0 copy-start.7
  158.8 3.0 %copy-start = (f32[512,256]{1,0:T(8,128)S(1)}, f32[512,256]{1,0:T(8,128)}, u32[]{:S(2)}) copy-start(f32[512,256]{1,0:T(8,128)} %param.15) | copy-start | bytes 1572868
where the time goes:
time: 163 us
  blocking collectives  135 us (83%)
  starting transfers between devices  8.69 us (5%)
  waiting for transfers between devices  7.11 us (4%)
  local copies, waits for them, and re-layouts  5.61 us (3%)
  other arithmetic  4.02 us (2%)
  between operations  2.72 us (2%)
    psum x1, blocking collectives, shards(): lax.psum((grad_blocks[0].astype(jnp.float32), ln_grads[0].astype(jnp.floa...  69.7 us
    psum x1, blocking collectives, shards(): lax.psum(squares(gradient, ln_gradient, row_count), ('row', 'col'))  64.9 us
    all_to_all x1, starting transfers between devices, shards(): lax.all_to_all(summed, 'col', split_axis=0, concat_axis=1, tiled=True)  4.96 us
    unnamed x22, local copies, waits for them, and re-layouts  4.42 us
    all_to_all x1, waiting for transfers between devices, shards(): lax.all_to_all(summed, 'col', split_axis=0, concat_axis=1, tiled=True)  4.12 us
    all_to_all x1, starting transfers between devices, shards(): lax.all_to_all(master_new, 'col', split_axis=1, concat_axis=0, tiled=True)  3.73 us
  transfers between devices with their start and end apart: 2, of which 2 were waited for; matrix products, arithmetic and copies ran while one was open for 3% of the time, Pallas kernels for 0%

commit v1 on v0

--- a/solution.py
+++ b/solution.py
@@ -54,7 +54,7 @@
         (grad_blocks[0].astype(jnp.float32), ln_grads[0].astype(jnp.float32)), "dp"
     )
     gradient = lax.all_to_all(summed, "col", split_axis=0, concat_axis=1, tiled=True)
-    norm_total = lax.psum(squares(gradient, ln_gradient, row_count), ("row", "col"))
+    norm_total = lax.psum(lax.psum(squares(gradient, ln_gradient, row_count), "row"), "col")
     clip_scale = clip_factor(norm_total)
     master_new, first_new, second_new = adam_step(
         gradient, clip_scale, first_moment, second_moment, master, decay_rate

time: 163 us -> 122 us (0.75)
  blocking collectives: 135 us -> 92.4 us
    psum x1 -> x2, blocking collectives: 64.9 us -> 22.8 us  [the longest x1 12.9 us: shards(): lax.psum(squares(gradient, ln_gradient, row_count), 'row')]
  transfers between devices with their start and end apart: 2 -> 2, of which waited for: 2 -> 2; matrix products, arithmetic and copies ran while one was open for 3% -> 4% of each run, Pallas kernels for 0% -> 0%
where the time goes in v1:
time: 122 us
  blocking collectives  92.4 us (76%)
  starting transfers between devices  9.57 us (8%)
  waiting for transfers between devices  8.15 us (7%)
  local copies, waits for them, and re-layouts  4.77 us (4%)
  other arithmetic  4.02 us (3%)
  between operations  2.73 us (2%)
    psum x1, blocking collectives, shards(): lax.psum((grad_blocks[0].astype(jnp.float32), ln_grads[0].astype(jnp.floa...  69.7 us
    psum x1, blocking collectives, shards(): lax.psum(squares(gradient, ln_gradient, row_count), 'row')  12.9 us
    psum x1, blocking collectives, shards(): lax.psum(lax.psum(squares(gradient, ln_gradient, row_count), 'row'), 'col')  9.83 us
    all_to_all x1, waiting for transfers between devices, shards(): lax.all_to_all(summed, 'col', split_axis=0, concat_axis=1, tiled=True)  5.16 us
    all_to_all x1, starting transfers between devices, shards(): lax.all_to_all(summed, 'col', split_axis=0, concat_axis=1, tiled=True)  4.96 us
    all_to_all x1, starting transfers between devices, shards(): lax.all_to_all(master_new, 'col', split_axis=1, concat_axis=0, tiled=True)  4.61 us
    unnamed x22, local copies, waits for them, and re-layouts  3.59 us
    all_to_all x1, waiting for transfers between devices, shards(): lax.all_to_all(master_new, 'col', split_axis=1, concat_axis=0, tiled=True)  2.99 us
  transfers between devices with their start and end apart: 2, of which 2 were waited for; matrix products, arithmetic and copies ran while one was open for 4% of the time, Pallas kernels for 0%

profile of v1, /device:TPU:2, one launch (start us, length us, event | category | flops | bytes accessed | tf_op | source)
XLA Modules:
  0.0 121.7 jit_solution(5111033221474900898)
XLA Ops:
  0.6 0.7 bitcast_convert_fusion
  1.3 69.7 %all-reduce.2 = (f32[4,128,256]{2,1,0:T(8,128)}, f32[4,256]{1,0:T(4,128)S(1)}) all-reduce(bf16[4,128,256]{2,1,0:T(8,128)(2,1)} %bitcast.20, f32[4,256]{1,0:T(4,128)S(1)} %bitcast_convert_fusion), channel_id=1, replica_groups=mesh['dp'=16,'row'=8,'col'=4] {'dp'}, use_global_device_ids=true, to_apply=%region_0.0 | all-reduce | flops 132096 | bytes 794624 | tf_op jit(solution)/shard_map/psum | solution.py:53
  71.0 5.0 %all-to-all-start = ((f32[4,128,256]{2,1,0:T(8,128)}), f32[4,128,256]{2,1,0:T(8,128)S(1)}, u32[]{:S(2)}, u32[]{:S(2)}) async-start(f32[4,128,256]{2,1,0:T(8,128)} %get-tuple-element.16), calls=%async_computation | async-start | bytes 1048576 | tf_op jit(solution)/shard_map/all_to_all | solution.py:56
  76.0 0.2 copy.24
  76.2 0.0 copy-start.2
  76.2 0.6 multiply_reduce_fusion.1
  77.4 5.2 %all-to-all-done = f32[4,128,256]{2,1,0:T(8,128)S(1)} async-done(((f32[4,128,256]{2,1,0:T(8,128)}), f32[4,128,256]{2,1,0:T(8,128)S(1)}, u32[]{:S(2)}, u32[]{:S(2)}) %all-to-all-start) | async-done | bytes 524320 | tf_op jit(solution)/shard_map/all_to_all | solution.py:56
  82.6 0.7 multiply_reduce_fusion
  84.0 0.0 copy-start.3
  84.0 0.2 copy.20
  84.2 12.9 %psum.30 = f32[]{:T(128)} all-reduce(f32[]{:T(128)S(6)} %add.47), channel_id=1, replica_groups=mesh['dp'=16,'row'=8,'col'=4] {'row'}, use_global_device_ids=true, to_apply=%region_4.0 | all-reduce | flops 1 | bytes 8 | tf_op jit(solution)/shard_map/psum | solution.py:57
  97.1 0.2 copy.22
  97.3 9.8 %psum.31 = f32[]{:T(128)} all-reduce(f32[]{:T(128)} %psum.30), channel_id=1, replica_groups=mesh['dp'=16,'row'=8,'col'=4] {'col'}, use_global_device_ids=true, to_apply=%region_5.0 | all-reduce | flops 1 | bytes 8 | tf_op jit(solution)/shard_map/psum | solution.py:57
  107.8 0.2 copy.21
  108.1 0.4 multiply_subtract_fusion
  108.5 1.0 copy.25
  109.5 4.6 %all-to-all-start.1 = ((f32[128,4,256]{2,0,1:T(8,128)}), f32[128,4,256]{2,0,1:T(8,128)S(1)}, u32[]{:S(2)}, u32[]{:S(2)}) async-start(f32[128,4,256]{2,0,1:T(8,128)} %copy.25), calls=%async_computation.1 | async-start | bytes 1048576 | tf_op jit(solution)/shard_map/all_to_all | solution.py:66
  114.1 1.0 copy.26
  115.1 1.0 copy.27
  116.1 1.0 copy.28
  117.1 0.0 copy-done.5
  117.1 0.6 multiply_add_fusion
  117.7 3.0 %all-to-all-done.1 = f32[128,4,256]{2,0,1:T(8,128)S(1)} async-done(((f32[128,4,256]{2,0,1:T(8,128)}), f32[128,4,256]{2,0,1:T(8,128)S(1)}, u32[]{:S(2)}, u32[]{:S(2)}) %all-to-all-start.1) | async-done | bytes 524320 | tf_op jit(solution)/shard_map/all_to_all | solution.py:66
  120.8 0.9 bitcast_add_fusion
  (15 shorter events, 0.1 us)
Async XLA Ops:
  71.0 5.0 %copy-start.1 = (f32[128,1024]{1,0:T(8,128)S(1)}, f32[128,1024]{1,0:T(8,128)}, u32[]{:S(2)}) copy-start(f32[128,1024]{1,0:T(8,128)} %param.12) | copy-start | bytes 1572868
  71.0 11.6 %all-to-all-start = ((f32[4,128,256]{2,1,0:T(8,128)}), f32[4,128,256]{2,1,0:T(8,128)S(1)}, u32[]{:S(2)}, u32[]{:S(2)}) async-start(f32[4,128,256]{2,1,0:T(8,128)} %get-tuple-element.16), calls=%async_computation | async-start | bytes 1048576 | tf_op jit(solution)/shard_map/all_to_all | solution.py:56
  76.2 7.8 %copy-start.2 = (f32[128,1024]{1,0:T(8,128)S(1)}, f32[128,1024]{1,0:T(8,128)}, u32[]{:S(2)}) copy-start(f32[128,1024]{1,0:T(8,128)} %param.13) | copy-start | bytes 1572868
  84.0 13.1 %copy-start.3 = (f32[128,1024]{1,0:T(8,128)S(1)}, f32[128,1024]{1,0:T(8,128)}, u32[]{:S(2)}) copy-start(f32[128,1024]{1,0:T(8,128)} %param.14) | copy-start | bytes 1572868
  109.5 11.2 %all-to-all-start.1 = ((f32[128,4,256]{2,0,1:T(8,128)}), f32[128,4,256]{2,0,1:T(8,128)S(1)}, u32[]{:S(2)}, u32[]{:S(2)}) async-start(f32[128,4,256]{2,0,1:T(8,128)} %copy.25), calls=%async_computation.1 | async-start | bytes 1048576 | tf_op jit(solution)/shard_map/all_to_all | solution.py:66
  116.1 1.0 copy-start.4
  116.1 1.0 copy-start.5
  116.1 1.0 copy-start.6
  116.1 1.0 copy-start.7
  117.7 3.0 %copy-start = (f32[512,256]{1,0:T(8,128)S(1)}, f32[512,256]{1,0:T(8,128)}, u32[]{:S(2)}) copy-start(f32[512,256]{1,0:T(8,128)} %param.15) | copy-start | bytes 1572868
